TPU v7x, 32 devices: a whole 2x2x4 slice. The times are simulated.
32 devices in a mesh: parts: 2 (over x), ctx: 8 (over z, y), head: 2 (over core).
Axes of the slice: x: 2, y: 2, z: 4, core: 2. Of those that a mesh axis runs over, the one named last changes fastest.
Arguments:
- channels: bfloat16 [2048, 2048], P(('parts', 'ctx'), 'head'), parts along dimension 0, may hold values from -6 to 6
- gate_channels: bfloat16 [2048, 2048], P(('parts', 'ctx'), 'head'), parts along dimension 0, may hold values from -6 to 6
- bmat: bfloat16 [2048, 512], P(('parts', 'ctx'), 'head'), parts along dimension 0, may hold values from -4 to 4
- cmat: bfloat16 [2048, 512], P(('parts', 'ctx'), 'head'), parts along dimension 0, may hold values from -4 to 4
- dt: float32 [2048, 32], P(('parts', 'ctx'), 'head'), parts along dimension 0, may hold values from 0.1 to 40
- rates: float32 [32], P('head'), may hold values from 0.00029296876 to 0.03
- skip: float32 [32], P('head'), may hold values from 0.5 to 2
- norm_gain: float32 [2048], P('head'), may hold values from 0.25 to 1.75
- docs: int32 [2048], P(('parts', 'ctx')), parts along dimension 0, may hold values from 0 to 3, never falling along the last dimension, each value on 1 to 512 neighbouring positions
- w_out: bfloat16 [2048, 2688], P('head', 'ctx'), may hold values from -0.125 to 0.125
- residual: bfloat16 [2048, 2688], P(('parts', 'ctx', 'head')), parts along dimension 0, may hold values from -6 to 6
- moe_gain: float32 [2688], replicated, may hold values from 0.25 to 1.75
- experts: int32 [2048, 6], P(('parts', 'ctx', 'head')), parts along dimension 0, may hold values from 0 to 15, all different within a row; in each aligned block of 64 rows (0 to 63, 64 to 127, ...) at most 36 rows name the same one
- gates: float32 [2048, 6], P(('parts', 'ctx', 'head')), parts along dimension 0, may hold values from 0.05 to 0.5
- w_up: bfloat16 [16, 2688, 928], P(('ctx', 'head')), may hold values from -0.125 to 0.125
- w_down: bfloat16 [16, 928, 2688], P(('ctx', 'head')), may hold values from -0.1875 to 0.1875
Outputs:
- layer_out: bfloat16 [2048, 2688], P(('parts', 'ctx', 'head')), parts along dimension 0
There are 2 independent parts, one for each index of `parts`. A program takes and returns all parts, laid end to end along the dimension named above; an argument that names none is the same for every part. Nothing has to cross between parts.
Inputs may be any that keep to these rules, and one draw needn't show every extreme that they name: Each row names 6 different experts; in each aligned block of 64 rows (the rows of one device) no expert is named by more than 36 rows. `docs`: ids never fall along the tokens; a document starts where the id changes and holds at most half of the 1024 tokens.
All inputs are finite; a program needn't handle non-finite values.
Results may differ from a plain program's by a relative error of at most 0.013.
Values may be sent and summed in bfloat16 or wider, within the bound.
No kernel may reach another device: no remote copies, remote signals or barrier semaphores. Data moves between devices by JAX's collectives and lax.ppermute only.
A program may use at most 128 MiB of HBM per device.

v0:
```python
import jax
import jax.numpy as jnp
from jax import lax
from jax.sharding import PartitionSpec as P

HEADS = 32
HEAD_DIM = 64
GROUPS = 4
STATE = 128
EPS = 1e-05


def entering(array, axis, combine, identity):
    size, place = (lax.axis_size(axis), lax.axis_index(axis))
    everything = jax.tree.map(lambda part: lax.all_gather(part, axis), array)
    start = jax.tree.map(
        lambda part, zero: jnp.broadcast_to(jnp.asarray(zero, part.dtype), part.shape),
        array,
        identity,
    )

    def lap(k, before):
        reached = k < place
        new = combine(before, jax.tree.map(lambda part: part[k], everything))
        return jax.tree.map(lambda a, b: jnp.where(reached, a, b), new, before)

    return lax.fori_loop(0, size, lap, start)


def silu(value):
    return value / (1.0 + jnp.exp(-value))


def combine_states(earlier, later):
    first_a, last_a, decay_a, state_a = earlier
    first_b, last_b, decay_b, state_b = later
    linked = ((last_a == first_b) | (last_a < 0) | (first_b < 0)).astype(jnp.float32)
    carried = decay_b * linked
    decay = carried * decay_a
    state = state_b + carried[:, None, None] * state_a
    first = jnp.where(first_a < 0, first_b, first_a)
    last = jnp.where(last_b < 0, last_a, last_b)
    return (first, last, decay, state)


def group_terms(inputs, causal, ending):
    x_group, b_group, c_group, log_group, dt_group = inputs
    scores = jnp.dot(c_group, b_group.T, preferred_element_type=jnp.float32)
    gap = jnp.where(causal[:, :, None], log_group[:, None, :] - log_group[None, :, :], -jnp.inf)
    weight = jnp.exp(gap) * scores[:, :, None] * dt_group[None, :, :]
    inner = jnp.einsum("tsh,shp->thp", weight, x_group, precision=lax.Precision.HIGHEST)
    tail = jnp.exp(log_group[-1][None, :] - log_group) * ending[:, None] * dt_group
    end_state = jnp.einsum(
        "sh,shp,sn->hpn",
        tail,
        x_group,
        b_group.astype(jnp.float32),
        precision=lax.Precision.HIGHEST,
    )
    return (inner, end_state)


def expert_rows(received, up_weight, down_weight):
    sources, items, width = received.shape
    rows = received.reshape(sources * items, width)
    up = jnp.dot(rows, up_weight, preferred_element_type=jnp.float32)
    act = jnp.square(jnp.maximum(up, 0.0)).astype(jnp.bfloat16)
    result = jnp.dot(act, down_weight, preferred_element_type=jnp.float32).astype(jnp.bfloat16)
    return result.reshape(sources, items, width)


def local(
    channels,
    gate_channels,
    bmat,
    cmat,
    dt,
    rates,
    skip,
    norm_gain,
    docs,
    w_out,
    residual,
    moe_gain,
    experts,
    gates,
    w_up,
    w_down,
):
    length = channels.shape[0]
    heads = dt.shape[1]
    groups = bmat.shape[1] // STATE
    per_group = heads // groups
    logs = jnp.cumsum(-rates[None, :] * dt, axis=0)
    x_wide = channels.astype(jnp.float32).reshape(length, groups, per_group, HEAD_DIM)
    b_split = bmat.reshape(length, groups, STATE)
    c_split = cmat.reshape(length, groups, STATE)
    position = jnp.arange(length, dtype=jnp.int32)
    causal = (docs[:, None] == docs[None, :]) & (position[:, None] >= position[None, :])
    ending = (docs == docs[length - 1]).astype(jnp.float32)
    opening = (docs == docs[0]).astype(jnp.float32)
    stacked = (
        x_wide.transpose(1, 0, 2, 3),
        b_split.transpose(1, 0, 2),
        c_split.transpose(1, 0, 2),
        logs.reshape(length, groups, per_group).transpose(1, 0, 2),
        dt.reshape(length, groups, per_group).transpose(1, 0, 2),
    )
    inner, end_state = lax.map(lambda item: group_terms(item, causal, ending), stacked)
    end_state = end_state.reshape(heads, HEAD_DIM, STATE)
    whole_decay = jnp.exp(logs[length - 1]) * (docs[0] == docs[length - 1]).astype(jnp.float32)
    element = (docs[:1], docs[length - 1 :], whole_decay, end_state)
    identity = (
        jnp.full((1,), -1, jnp.int32),
        jnp.full((1,), -1, jnp.int32),
        jnp.ones((heads,), jnp.float32),
        jnp.zeros_like(end_state),
    )
    _, prior_last, _, incoming = entering(element, "ctx", combine_states, identity)
    linked = (prior_last == docs[:1]).astype(jnp.float32)
    reach = jnp.exp(logs) * opening[:, None] * linked
    outer = jnp.einsum(
        "tgn,ghpn->tghp",
        c_split.astype(jnp.float32),
        incoming.reshape(groups, per_group, HEAD_DIM, STATE),
        precision=lax.Precision.HIGHEST,
    )
    outer = outer * reach.reshape(length, groups, per_group)[:, :, :, None]
    inner = inner.transpose(1, 0, 2, 3)
    scan = (inner + outer).reshape(length, heads, HEAD_DIM) + skip[None, :, None] * x_wide.reshape(
        length, heads, HEAD_DIM
    )
    scan = scan.reshape(length, heads * HEAD_DIM)
    gated = scan * silu(gate_channels.astype(jnp.float32))
    grouped = gated.reshape(length, -1, HEADS * HEAD_DIM // GROUPS)
    grouped = grouped / jnp.sqrt(jnp.mean(grouped * grouped, axis=2, keepdims=True) + EPS)
    normed_scan = (grouped.reshape(length, -1) * norm_gain).astype(jnp.bfloat16)
    partial_value = jnp.dot(
        normed_scan,
        lax.all_gather(w_out, "ctx", axis=1, tiled=True),
        preferred_element_type=jnp.float32,
    )
    mamba_out = lax.psum_scatter(
        partial_value.astype(jnp.bfloat16), "head", scatter_dimension=0, tiled=True
    ).astype(jnp.float32)
    hidden = (residual.astype(jnp.float32) + mamba_out).astype(jnp.bfloat16)
    widened = hidden.astype(jnp.float32)
    moe_in = (
        widened / jnp.sqrt(jnp.mean(widened * widened, axis=1, keepdims=True) + EPS) * moe_gain
    ).astype(jnp.bfloat16)
    rows_dev = moe_in.shape[0]
    top = experts.shape[1]
    width = moe_in.shape[1]
    ctx_count = lax.axis_size("ctx")
    head_count = lax.axis_size("head")
    experts_all = ctx_count * head_count
    capacity = min(rows_dev, max(4, 3 * rows_dev * top // (2 * experts_all)))
    picks = experts.reshape(-1)
    pick_index = jnp.arange(picks.shape[0], dtype=jnp.int32)
    earlier = (picks[:, None] == picks[None, :]) & (pick_index[None, :] < pick_index[:, None])
    slot = jnp.sum(earlier.astype(jnp.int32), axis=1)
    target = (picks * capacity + slot).reshape(rows_dev, top)
    places = jnp.arange(experts_all * capacity, dtype=jnp.int32)
    routing = jnp.any(target[None, :, :] == places[:, None, None], axis=2).astype(jnp.bfloat16)
    outgoing = jnp.dot(routing, moe_in, preferred_element_type=jnp.float32).astype(jnp.bfloat16)
    outgoing = outgoing.reshape(experts_all, capacity, width)
    up_weight = w_up[0]
    down_weight = w_down[0]
    results = expert_rows(
        lax.all_to_all(outgoing, ("ctx", "head"), split_axis=0, concat_axis=0, tiled=True),
        up_weight,
        down_weight,
    )
    returned = lax.all_to_all(results, ("ctx", "head"), split_axis=0, concat_axis=0, tiled=True)
    flat_back = returned.reshape(experts_all * capacity, width)
    chosen = flat_back[target].astype(jnp.float32)
    mixture = jnp.sum(chosen * gates[:, :, None], axis=1)
    return (widened + mixture).astype(jnp.bfloat16)


def solution(mesh):
    return jax.shard_map(
        local,
        mesh=mesh,
        in_specs=(
            P(("parts", "ctx"), "head"),
            P(("parts", "ctx"), "head"),
            P(("parts", "ctx"), "head"),
            P(("parts", "ctx"), "head"),
            P(("parts", "ctx"), "head"),
            P("head"),
            P("head"),
            P("head"),
            P(("parts", "ctx")),
            P("head", "ctx"),
            P(("parts", "ctx", "head"), None),
            P(),
            P(("parts", "ctx", "head"), None),
            P(("parts", "ctx", "head"), None),
            P(("ctx", "head"), None, None),
            P(("ctx", "head"), None, None),
        ),
        out_specs=P(("parts", "ctx", "head"), None),
        check_vma=False,
    )
```

profile of v0, /device:TPU:13, one launch (start us, length us, event | category | flops | bytes accessed | tf_op | source)
XLA Modules:
  0.0 410.6 jit_solution(10175892320558822707)
XLA Ops:
  12.6 1.9 fusion.64
  14.5 1.8 compare_convert_fusion
  16.2 6.9 %while.29 = (s32[]{:T(128)}, f32[2,128,8,64]{1,3,2,0:T(8,128)S(1)}, f32[2,8,64,128]{3,2,1,0:T(8,128)S(1)}, f32[2,128,8,64]{1,3,2,0:T(8,128)S(1)}, f32[2,128,8]{1...) while((s32[]{:T(128)}, f32[2,128,8,64]{1,3,2,0:T(8,128)S(1)}, ...), condition=%wide.region_2.3_spmd.clone, body=%wide.region_1.2_spmd.clone.sunk | while | flops 206162944 | bytes 1364697 | solution.py:109
  24.8 1.4 slice_dynamic-update-slice_fusion
  26.2 7.9 %all-reduce.2 = (s32[8]{0:T(128)S(1)}, s32[8]{0:T(128)S(1)}) all-reduce(s32[8]{0:T(128)S(1)} %get-tuple-element.359, s32[8]{0:T(128)S(1)} %slice_dynamic-update-slice_fusion), channel_id=2, replica_groups=mesh['parts'=2,'ctx'=8,'head'=2] {'ctx'}, use_global_device_ids=true, to_apply=%add | all-reduce | flops 16 | bytes 128
  35.3 12.1 %all-gather.2 = f32[8,1,16]{2,1,0:T(1,128)S(1)} all-gather(f32[1,1,16]{2,1,0:T(1,128)S(1)} %fusion.61), channel_id=1, replica_groups=mesh['parts'=2,'ctx'=8,'head'=2] {'ctx'}, dimensions={0}, use_global_device_ids=true | all-gather | bytes 576 | tf_op jit(solution)/shard_map/all_gather | solution.py:15
  47.4 47.7 %all-gather.6.cloned.1.call-done = f32[8,16,64,128]{3,2,1,0:T(8,128)} async-done(((f32[1,16,64,128]{3,2,1,0:T(8,128)}), f32[8,16,64,128]{3,2,1,0:T(8,128)}) %all-gather.6.cloned.1.call-update) | async-done | bytes 4194320 | tf_op jit(solution)/shard_map/all_gather | solution.py:15
  95.1 35.5 %while.30 = (s32[]{:T(128)}, s32[1]{0:T(128)}, f32[16,64,128]{2,1,0:T(8,128)S(1)}, s32[]{:T(128)}, s32[8,1]{0,1:T(1,128)S(1)}, /*index=5*/f32[8,16,64,128]{3,2,1...) while((s32[]{:T(128)}, s32[1]{0:T(128)}, ...), condition=%wide.region_4.5_spmd.clone, body=%wide.region_3.4_spmd.clone.sunk | while | flops 524317 | bytes 1573290 | solution.py:27
  133.0 51.6 %all-gather.8.cloned.1.call-done = bf16[1024,2688]{0,1:T(8,128)(2,1)} async-done(((bf16[1024,336]{0,1:T(8,128)(2,1)}), bf16[1024,2688]{0,1:T(8,128)(2,1)}) %all-gather.8.cloned.1.call-update) | async-done | bytes 5505040 | tf_op jit(solution)/shard_map/all_gather | solution.py:140
  184.7 5.4 %convolution_convert_fusion.1 = bf16[128,2688]{1,0:T(8,128)(2,1)} fusion(bf16[1024,2688]{0,1:T(8,128)(2,1)} %all-gather.8.cloned.1.call-done, f32[128,1024]{1,0:T(8,128)S(1)} %bitcast.145, f32[1024]{0:T(1024)S(1)} %copy-done.10, bf16[128,1024]{1,0:T(8,128)(2,1)S(1)} %copy-done.5, f32[128,1024]{1,0:T(8,128)S(1)} %copy.99, f32[1024]{0:T(1024)S(1)} %mul.206, ...), kind=kOutput, calls=%fused_computation.53 | convolution fusion | flops 706428928 | bytes 7774208 | tf_op jit(solution)/shard_map/dot_general | solution.py:138
  191.0 9.5 %reduce-scatter.2.cloned.1.call-done = bf16[64,2688]{1,0:T(8,128)(2,1)} async-done(((bf16[128,2688]{1,0:T(8,128)(2,1)}), bf16[64,2688]{1,0:T(8,128)(2,1)}) %reduce-scatter.2.cloned.1.call-update) | async-done | bytes 344080 | tf_op jit(solution)/shard_map/reduce_scatter | solution.py:143
  201.7 2.0 convolution_convert_fusion
  203.8 2.5 reshape.115
  206.2 81.9 %all_to_all.10 = bf16[16,36,2688]{2,1,0:T(8,128)(2,1)S(1)} all-to-all(bf16[16,36,2688]{2,1,0:T(8,128)(2,1)} %reshape.115), channel_id=1, replica_groups=mesh['parts'=2,'ctx'=8,'head'=2] {'ctx','head'}, dimensions={0} | all-to-all | bytes 6193152 | tf_op jit(solution)/shard_map/all_to_all | solution.py:170
  288.1 2.4 reshape.116
  290.5 6.9 %multiply_convert_fusion = bf16[576,928]{1,0:T(8,128)(2,1)S(1)} fusion(bf16[576,2688]{1,0:T(8,128)(2,1)} %reshape.116, bf16[1,2688,928]{1,2,0:T(8,128)(2,1)} %param.34), kind=kOutput, calls=%fused_computation.54 | convolution fusion | flops 2875226112 | bytes 9154560 | tf_op jit(solution)/shard_map/dot_general | solution.py:66
  297.4 6.2 %fusion.38 = bf16[576,2688]{1,0:T(8,128)(2,1)S(1)} fusion(bf16[576,928]{1,0:T(8,128)(2,1)S(1)} %multiply_convert_fusion, bf16[1,928,2688]{2,1,0:T(8,128)(2,1)} %param.35), kind=kOutput, calls=%fused_computation.51 | convolution fusion | flops 2875170816 | bytes 9154560 | tf_op jit(solution)/shard_map/dot_general | solution.py:68
  303.5 2.5 reshape.117
  306.1 5.3 %all-to-all-start.1 = ((bf16[16,36,2688]{2,1,0:T(8,128)(2,1)}), bf16[16,36,2688]{2,1,0:T(8,128)(2,1)}, u32[]{:S(2)}, u32[]{:S(2)}) async-start(bf16[16,36,2688]{2,1,0:T(8,128)(2,1)} %reshape.117), calls=%async_computation.2 | async-start | bytes 6881280 | tf_op jit(solution)/shard_map/all_to_all | solution.py:174
  311.7 76.0 %all-to-all-done.1 = bf16[16,36,2688]{2,1,0:T(8,128)(2,1)} async-done(((bf16[16,36,2688]{2,1,0:T(8,128)(2,1)}), bf16[16,36,2688]{2,1,0:T(8,128)(2,1)}, u32[]{:S(2)}, u32[]{:S(2)}) %all-to-all-start.1) | async-done | bytes 3096608 | tf_op jit(solution)/shard_map/all_to_all | solution.py:174
  387.7 3.0 reshape.118
  390.6 3.4 gather_fusion
  394.1 4.5 %reshape.133 = f32[64,6,2688]{2,1,0:T(8,128)} reshape(bf16[384,2688]{1,0:T(8,128)(2,1)} %gather_fusion) | data formatting | bytes 6193152 | tf_op jit(solution)/shard_map/convert_element_type | solution.py:176
  398.6 4.6 %multiply_reduce_fusion = f32[64,2688]{1,0:T(8,128)S(1)} fusion(f32[64,6,2688]{2,1,0:T(8,128)} %reshape.133, f32[64,6]{1,0:T(8,128)S(1)} %copy.105), kind=kLoop, calls=%fused_computation.46 | loop fusion | flops 1892352 | bytes 4818432 | tf_op jit(solution)/shard_map/reduce_sum | solution.py:177
  (108 shorter events, 34.5 us)
Async XLA Ops:
  6.5 88.6 %all-gather.6.cloned.1.call-start = ((), (), s32[]{:S(2)}) async-start(), calls=%async_computation.3 | async-start | bytes 4718592 | tf_op jit(solution)/shard_map/all_gather | solution.py:15
  16.2 18.9 %copy-start.9 = (f32[16]{0:T(128)S(1)}, f32[16]{0:T(128)}, u32[]{:S(2)}) copy-start(f32[16]{0:T(128)} %param.26) | copy-start | bytes 196
  23.2 0.8 copy-start.4
  24.0 160.7 %all-gather.8.cloned.1.call-start = ((), (), s32[]{:S(2)}) async-start(), calls=%async_computation.4 | async-start | bytes 6193152 | tf_op jit(solution)/shard_map/all_gather | solution.py:140
  24.7 175.8 %reduce-scatter.2.cloned.1.call-start = ((), (), s32[]{:S(2)}) async-start(), calls=%async_computation.5 | async-start | bytes 1032192 | tf_op jit(solution)/shard_map/reduce_scatter | solution.py:143
  95.1 36.7 %copy-start.3 = (bf16[128,1024]{1,0:T(8,128)(2,1)S(1)}, bf16[128,1024]{1,0:T(8,128)(2,1)}, u32[]{:S(2)}) copy-start(bf16[128,1024]{1,0:T(8,128)(2,1)} %param.20) | copy-start | bytes 786436
  95.1 36.7 %copy-start.5 = (bf16[128,1024]{1,0:T(8,128)(2,1)S(1)}, bf16[128,1024]{1,0:T(8,128)(2,1)}, u32[]{:S(2)}) copy-start(bf16[128,1024]{1,0:T(8,128)(2,1)} %param.21) | copy-start | bytes 786436
  131.2 53.4 %copy-start.10 = (f32[1024]{0:T(1024)S(1)}, f32[1024]{0:T(1024)}, u32[]{:S(2)}) copy-start(f32[1024]{0:T(1024)} %param.27) | copy-start | bytes 12292
  184.6 5.4 %copy-start.6 = (s32[64,6]{0,1:T(8,128)S(1)}, s32[64,6]{0,1:T(8,128)}, u32[]{:S(2)}) copy-start(s32[64,6]{0,1:T(8,128)} %param.32) | copy-start | bytes 4612
  184.6 15.9 %copy-start = (bf16[64,2688]{1,0:T(8,128)(2,1)S(1)}, bf16[64,2688]{1,0:T(8,128)(2,1)}, u32[]{:S(2)}) copy-start(bf16[64,2688]{1,0:T(8,128)(2,1)} %param.30) | copy-start | bytes 1032196
  184.6 17.1 %copy-start.7 = (f32[2688]{0:T(1024)S(1)}, f32[2688]{0:T(1024)}, u32[]{:S(2)}) copy-start(f32[2688]{0:T(1024)} %param.31) | copy-start | bytes 32260
  306.1 5.5 %copy-start.8 = (f32[64,6]{0,1:T(8,128)S(1)}, f32[64,6]{0,1:T(8,128)}, u32[]{:S(2)}) copy-start(f32[64,6]{0,1:T(8,128)} %param.33) | copy-start | bytes 4612
  306.1 81.6 %all-to-all-start.1 = ((bf16[16,36,2688]{2,1,0:T(8,128)(2,1)}), bf16[16,36,2688]{2,1,0:T(8,128)(2,1)}, u32[]{:S(2)}, u32[]{:S(2)}) async-start(bf16[16,36,2688]{2,1,0:T(8,128)(2,1)} %reshape.117), calls=%async_computation.2 | async-start | bytes 6881280 | tf_op jit(solution)/shard_map/all_to_all | solution.py:174
  398.6 4.6 %copy-start.1 = (bf16[64,2688]{1,0:T(8,128)(2,1)S(1)}, bf16[64,2688]{1,0:T(8,128)(2,1)}, u32[]{:S(2)}) copy-start(bf16[64,2688]{1,0:T(8,128)(2,1)} %param.30) | copy-start | bytes 1032196
  398.6 4.6 %copy-start.2 = (bf16[64,2688]{1,0:T(8,128)(2,1)S(1)}, bf16[64,2688]{1,0:T(8,128)(2,1)}, u32[]{:S(2)}) copy-start(bf16[64,2688]{1,0:T(8,128)(2,1)} %reduce-scatter.2.cloned.1.call-done) | copy-start | bytes 1032196
Sparse Core Ops, SparseCore 0:
  24.1 70.9 all-gather.5
  97.3 87.2 all-gather.7
  190.2 10.2 reduce-scatter.1
where the time goes:
time: 412 us; the launch traced here: 411 us
  waiting for transfers between devices  185 us (45%)
  blocking collectives  102 us (25%)
  local copies, waits for them, and re-layouts  34.4 us (8%)
  matrix products  24.1 us (6%)
  other arithmetic  23.5 us (6%)
  loops' own time  20.7 us (5%)
  between operations  15.1 us (4%)
  starting transfers between devices  5.37 us (1%)
    all_to_all x1, blocking collectives, local(): lax.all_to_all(outgoing, ('ctx', 'head'), split_axis=0, concat_axis=0, ti...  81.9 us
    all_to_all x1, waiting for transfers between devices, local(): lax.all_to_all(results, ('ctx', 'head'), split_axis=0, concat_axis=0, til...  76 us
    all_gather x1, waiting for transfers between devices, local(): lax.all_gather(w_out, 'ctx', axis=1, tiled=True)  51.6 us
    all_gather x1, waiting for transfers between devices, entering(): everything = jax.tree.map(lambda part: lax.all_gather(part, axis), array)  47.7 us
    another operation x1, loops' own time, entering(): return lax.fori_loop(0, size, lap, start)  20.6 us
    all_gather x1, blocking collectives, entering(): everything = jax.tree.map(lambda part: lax.all_gather(part, axis), array)  12.1 us
    reduce_scatter x1, waiting for transfers between devices, local(): lax.psum_scatter(partial_value.astype(jnp.bfloat16), 'head', scatter_dime...  9.49 us
    select_n x8, other arithmetic, lap(): return jax.tree.map(lambda a, b: jnp.where(reached, a, b), new, before)  9.42 us
  transfers between devices with their start and end apart: 4, of which 4 were waited for; matrix products, arithmetic and copies ran while one was open for 5% of the time, Pallas kernels for 0%

commit v1 on v0

--- a/solution.py
+++ b/solution.py
@@ -8,6 +8,11 @@
 GROUPS = 4
 STATE = 128
 EPS = 1e-05
+
+
+def gather_blocks(x, axis, d):
+    blocks = lax.all_gather(x, axis)
+    return jnp.concatenate(blocks, axis=d)
 
 
 def entering(array, axis, combine, identity):
@@ -136,9 +141,7 @@
     grouped = grouped / jnp.sqrt(jnp.mean(grouped * grouped, axis=2, keepdims=True) + EPS)
     normed_scan = (grouped.reshape(length, -1) * norm_gain).astype(jnp.bfloat16)
     partial_value = jnp.dot(
-        normed_scan,
-        lax.all_gather(w_out, "ctx", axis=1, tiled=True),
-        preferred_element_type=jnp.float32,
+        normed_scan, gather_blocks(w_out, "ctx", 1), preferred_element_type=jnp.float32
     )
     mamba_out = lax.psum_scatter(
         partial_value.astype(jnp.bfloat16), "head", scatter_dimension=0, tiled=True

time: 412 us -> 422 us (1.024)
  local copies, waits for them, and re-layouts: 34.4 us -> 46 us
    unnamed x31 -> x32, local copies, waits for them, and re-layouts: 5.67 us -> 14.6 us
where the time goes in v1:
time: 422 us; the launch traced here: 420 us
  waiting for transfers between devices  187 us (44%)
  blocking collectives  102 us (24%)
  local copies, waits for them, and re-layouts  46 us (11%)
  other arithmetic  23.6 us (6%)
  matrix products  21.8 us (5%)
  loops' own time  19.6 us (5%)
  between operations  15.1 us (4%)
  starting transfers between devices  5.37 us (1%)
    all_to_all x1, blocking collectives, local(): lax.all_to_all(outgoing, ('ctx', 'head'), split_axis=0, concat_axis=0, ti...  81.9 us
    all_to_all x1, waiting for transfers between devices, local(): lax.all_to_all(results, ('ctx', 'head'), split_axis=0, concat_axis=0, til...  76 us
    all_gather x1, waiting for transfers between devices, gather_blocks(): blocks = lax.all_gather(x, axis)  53 us
    all_gather x1, waiting for transfers between devices, entering(): everything = jax.tree.map(lambda part: lax.all_gather(part, axis), array)  47.7 us
    another operation x1, loops' own time, entering(): return lax.fori_loop(0, size, lap, start)  19.5 us
    unnamed x32, local copies, waits for them, and re-layouts  14.6 us
    all_gather x1, blocking collectives, entering(): everything = jax.tree.map(lambda part: lax.all_gather(part, axis), array)  12.1 us
    reduce_scatter x1, waiting for transfers between devices, local(): lax.psum_scatter(partial_value.astype(jnp.bfloat16), 'head', scatter_dime...  9.49 us
  transfers between devices with their start and end apart: 4, of which 4 were waited for; matrix products, arithmetic and copies ran while one was open for 5% of the time, Pallas kernels for 0%

profile of v1, /device:TPU:13, one launch (start us, length us, event | category | flops | bytes accessed | tf_op | source)
XLA Modules:
  0.0 420.2 jit_solution(17152976964112434941)
XLA Ops:
  12.6 1.9 fusion.64
  16.2 6.9 %while.29 = (s32[]{:T(128)}, f32[2,128,8,64]{1,3,2,0:T(8,128)S(1)}, f32[2,8,64,128]{3,2,1,0:T(8,128)S(1)}, f32[2,128,8,64]{1,3,2,0:T(8,128)S(1)}, f32[2,128,8]{1...) while((s32[]{:T(128)}, f32[2,128,8,64]{1,3,2,0:T(8,128)S(1)}, ...), condition=%wide.region_2.3_spmd.clone, body=%wide.region_1.2_spmd.clone.sunk | while | flops 206162944 | bytes 1364705 | solution.py:114
  26.2 7.9 %all-reduce.2 = (s32[8]{0:T(128)S(1)}, s32[8]{0:T(128)S(1)}) all-reduce(s32[8]{0:T(128)S(1)} %get-tuple-element.359, s32[8]{0:T(128)S(1)} %slice_dynamic-update-slice_fusion), channel_id=2, replica_groups=mesh['parts'=2,'ctx'=8,'head'=2] {'ctx'}, use_global_device_ids=true, to_apply=%add | all-reduce | flops 16 | bytes 128
  35.3 12.1 %all-gather.3 = f32[8,1,16]{2,1,0:T(1,128)S(1)} all-gather(f32[1,1,16]{2,1,0:T(1,128)S(1)} %fusion.61), channel_id=1, replica_groups=mesh['parts'=2,'ctx'=8,'head'=2] {'ctx'}, dimensions={0}, use_global_device_ids=true | all-gather | bytes 576 | tf_op jit(solution)/shard_map/all_gather | solution.py:20
  47.4 47.7 %all-gather.7.cloned.1.call-done = f32[8,16,64,128]{3,2,1,0:T(8,128)} async-done(((f32[1,16,64,128]{3,2,1,0:T(8,128)}), f32[8,16,64,128]{3,2,1,0:T(8,128)}) %all-gather.7.cloned.1.call-update) | async-done | bytes 4194320 | tf_op jit(solution)/shard_map/all_gather | solution.py:20
  95.1 34.1 %while.30 = (s32[]{:T(128)}, s32[1]{0:T(128)}, f32[16,64,128]{2,1,0:T(8,128)S(1)}, s32[]{:T(128)}, s32[8,1]{0,1:T(1,128)S(1)}, /*index=5*/f32[8,16,64,128]{3,2,1...) while((s32[]{:T(128)}, s32[1]{0:T(128)}, ...), condition=%wide.region_4.5_spmd.clone, body=%wide.region_3.4_spmd.clone.sunk | while | flops 524317 | bytes 1573298 | solution.py:32
  131.6 53.0 %all-gather.9.cloned.1.call-done = bf16[8192,336]{0,1:T(8,128)(2,1)} async-done(((bf16[1024,336]{0,1:T(8,128)(2,1)}), bf16[8192,336]{0,1:T(8,128)(2,1)}) %all-gather.9.cloned.1.call-update) | async-done | bytes 5505040 | tf_op jit(solution)/shard_map/all_gather | solution.py:14
  184.6 8.9 %copy.117 = bf16[42,8,8,1024]{3,2,1,0:T(8,128)(2,1)S(1)} copy(bf16[42,8,8,1024]{3,1,2,0:T(8,128)(2,1)} %bitcast.145) | data formatting | bytes 11010048
  193.5 3.1 copy.106
  196.7 3.0 convolution_convert_fusion.1
  200.7 9.5 %reduce-scatter.2.cloned.1.call-done = bf16[64,2688]{1,0:T(8,128)(2,1)} async-done(((bf16[128,2688]{1,0:T(8,128)(2,1)}), bf16[64,2688]{1,0:T(8,128)(2,1)}) %reduce-scatter.2.cloned.1.call-update) | async-done | bytes 344080 | tf_op jit(solution)/shard_map/reduce_scatter | solution.py:146
  211.4 2.0 convolution_convert_fusion
  213.4 2.5 reshape.123
  215.9 81.9 %all_to_all.10 = bf16[16,36,2688]{2,1,0:T(8,128)(2,1)S(1)} all-to-all(bf16[16,36,2688]{2,1,0:T(8,128)(2,1)} %reshape.123), channel_id=1, replica_groups=mesh['parts'=2,'ctx'=8,'head'=2] {'ctx','head'}, dimensions={0} | all-to-all | bytes 6193152 | tf_op jit(solution)/shard_map/all_to_all | solution.py:173
  297.7 2.4 reshape.124
  300.1 6.9 %multiply_convert_fusion = bf16[576,928]{1,0:T(8,128)(2,1)S(1)} fusion(bf16[576,2688]{1,0:T(8,128)(2,1)} %reshape.124, bf16[1,2688,928]{1,2,0:T(8,128)(2,1)} %param.34), kind=kOutput, calls=%fused_computation.54 | convolution fusion | flops 2875226112 | bytes 9154560 | tf_op jit(solution)/shard_map/dot_general | solution.py:71
  307.0 6.2 %fusion.38 = bf16[576,2688]{1,0:T(8,128)(2,1)S(1)} fusion(bf16[576,928]{1,0:T(8,128)(2,1)S(1)} %multiply_convert_fusion, bf16[1,928,2688]{2,1,0:T(8,128)(2,1)} %param.35), kind=kOutput, calls=%fused_computation.51 | convolution fusion | flops 2875170816 | bytes 9154560 | tf_op jit(solution)/shard_map/dot_general | solution.py:73
  313.2 2.5 reshape.125
  315.7 5.3 %all-to-all-start.1 = ((bf16[16,36,2688]{2,1,0:T(8,128)(2,1)}), bf16[16,36,2688]{2,1,0:T(8,128)(2,1)}, u32[]{:S(2)}, u32[]{:S(2)}) async-start(bf16[16,36,2688]{2,1,0:T(8,128)(2,1)} %reshape.125), calls=%async_computation.2 | async-start | bytes 6881280 | tf_op jit(solution)/shard_map/all_to_all | solution.py:177
  321.4 76.0 %all-to-all-done.1 = bf16[16,36,2688]{2,1,0:T(8,128)(2,1)} async-done(((bf16[16,36,2688]{2,1,0:T(8,128)(2,1)}), bf16[16,36,2688]{2,1,0:T(8,128)(2,1)}, u32[]{:S(2)}, u32[]{:S(2)}) %all-to-all-start.1) | async-done | bytes 3096608 | tf_op jit(solution)/shard_map/all_to_all | solution.py:177
  397.3 3.0 reshape.126
  400.3 3.4 gather_fusion
  403.7 4.5 %reshape.142 = f32[64,6,2688]{2,1,0:T(8,128)} reshape(bf16[384,2688]{1,0:T(8,128)(2,1)} %gather_fusion) | data formatting | bytes 6193152 | tf_op jit(solution)/shard_map/convert_element_type | solution.py:179
  408.3 4.6 %multiply_reduce_fusion = f32[64,2688]{1,0:T(8,128)S(1)} fusion(f32[64,6,2688]{2,1,0:T(8,128)} %reshape.142, f32[64,6]{1,0:T(8,128)S(1)} %copy.110), kind=kLoop, calls=%fused_computation.46 | loop fusion | flops 1892352 | bytes 4818432 | tf_op jit(solution)/shard_map/reduce_sum | solution.py:180
  (110 shorter events, 37.3 us)
Async XLA Ops:
  6.5 88.6 %all-gather.7.cloned.1.call-start = ((), (), s32[]{:S(2)}) async-start(), calls=%async_computation.3 | async-start | bytes 4718592 | tf_op jit(solution)/shard_map/all_gather | solution.py:20
  16.2 18.9 %copy-start.9 = (f32[16]{0:T(128)S(1)}, f32[16]{0:T(128)}, u32[]{:S(2)}) copy-start(f32[16]{0:T(128)} %param.26) | copy-start | bytes 196
  23.2 0.8 copy-start.4
  24.0 160.6 %all-gather.9.cloned.1.call-start = ((), (), s32[]{:S(2)}) async-start(), calls=%async_computation.5 | async-start | bytes 6193152 | tf_op jit(solution)/shard_map/all_gather | solution.py:14
  24.7 185.4 %reduce-scatter.2.cloned.1.call-start = ((), (), s32[]{:S(2)}) async-start(), calls=%async_computation.4 | async-start | bytes 1032192 | tf_op jit(solution)/shard_map/reduce_scatter | solution.py:146
  95.1 35.2 %copy-start.3 = (bf16[128,1024]{1,0:T(8,128)(2,1)S(1)}, bf16[128,1024]{1,0:T(8,128)(2,1)}, u32[]{:S(2)}) copy-start(bf16[128,1024]{1,0:T(8,128)(2,1)} %param.20) | copy-start | bytes 786436
  95.1 35.3 %copy-start.5 = (bf16[128,1024]{1,0:T(8,128)(2,1)S(1)}, bf16[128,1024]{1,0:T(8,128)(2,1)}, u32[]{:S(2)}) copy-start(bf16[128,1024]{1,0:T(8,128)(2,1)} %param.21) | copy-start | bytes 786436
  193.5 3.1 copy-start.10
  196.6 3.1 copy-start.6
  196.6 13.5 %copy-start = (bf16[64,2688]{1,0:T(8,128)(2,1)S(1)}, bf16[64,2688]{1,0:T(8,128)(2,1)}, u32[]{:S(2)}) copy-start(bf16[64,2688]{1,0:T(8,128)(2,1)} %param.30) | copy-start | bytes 1032196
  196.7 14.7 %copy-start.7 = (f32[2688]{0:T(1024)S(1)}, f32[2688]{0:T(1024)}, u32[]{:S(2)}) copy-start(f32[2688]{0:T(1024)} %param.31) | copy-start | bytes 32260
  315.7 5.3 %copy-start.8 = (f32[64,6]{0,1:T(8,128)S(1)}, f32[64,6]{0,1:T(8,128)}, u32[]{:S(2)}) copy-start(f32[64,6]{0,1:T(8,128)} %param.33) | copy-start | bytes 4612
  315.7 81.6 %all-to-all-start.1 = ((bf16[16,36,2688]{2,1,0:T(8,128)(2,1)}), bf16[16,36,2688]{2,1,0:T(8,128)(2,1)}, u32[]{:S(2)}, u32[]{:S(2)}) async-start(bf16[16,36,2688]{2,1,0:T(8,128)(2,1)} %reshape.125), calls=%async_computation.2 | async-start | bytes 6881280 | tf_op jit(solution)/shard_map/all_to_all | solution.py:177
  408.3 4.6 %copy-start.1 = (bf16[64,2688]{1,0:T(8,128)(2,1)S(1)}, bf16[64,2688]{1,0:T(8,128)(2,1)}, u32[]{:S(2)}) copy-start(bf16[64,2688]{1,0:T(8,128)(2,1)} %param.30) | copy-start | bytes 1032196
  408.3 4.6 %copy-start.2 = (bf16[64,2688]{1,0:T(8,128)(2,1)S(1)}, bf16[64,2688]{1,0:T(8,128)(2,1)}, u32[]{:S(2)}) copy-start(bf16[64,2688]{1,0:T(8,128)(2,1)} %reduce-scatter.2.cloned.1.call-done) | copy-start | bytes 1032196
Sparse Core Ops, SparseCore 0:
  24.1 70.9 all-gather.6
  97.3 87.2 all-gather.8
  199.8 10.2 reduce-scatter.1
